TPU v7x, 512 devices: a whole 4x4x16 slice. The times are simulated.
512 devices in a mesh: dp: 8 (over z_hi, y), shard: 64 (over x, z_lo, core).
Axes of the slice: x: 4, y: 4, z: 16 (z_hi: 2, z_lo: 8; z = z_hi * 8 + z_lo), core: 2. Of those that a mesh axis runs over, the one named last changes fastest.
Arguments:
- context: bfloat16 [8192, 4096], P('shard'), may hold values from -16 to 16
- projected: bfloat16 [8192, 4096], P('shard', 'dp'), may hold values from -6 to 6
- cotangent: bfloat16 [8192, 4096], P('shard', 'dp'), may hold values from -16 to 16
- modality: int32 [8192], P('shard'), may hold values from 0 to 2
- out_weight: bfloat16 [4096, 3, 4096], P('shard', None, 'dp'), may hold values from -0.09375 to 0.09375
- out_gain: float32 [3, 4096], P(None, 'dp'), may hold values from 0.25 to 1.75
Outputs:
- grad_context: bfloat16 [8192, 4096], P('shard', 'dp')
- grad_weight: float32 [4096, 3, 4096], P('shard', None, 'dp')
- grad_gain: float32 [3, 4096], P(None, 'dp')
All inputs are finite; a program needn't handle non-finite values.
Results may differ from a plain program's by a relative error of at most 0.0049.
Values may be sent and summed in bfloat16 or wider, within the bound.
No kernel may reach another device: no remote copies, remote signals or barrier semaphores. Data moves between devices by JAX's collectives and lax.ppermute only.
A program may use at most 64 MiB of HBM per device.

v0:
```python
import jax
import jax.numpy as jnp
from jax import lax
from jax.sharding import Mesh
from jax.sharding import PartitionSpec as P

D = 4096
DP = ("dp_0", "dp_1")
EPS = 1e-06


def from_everyone(shard, axis):
    count = lax.axis_size(axis)
    return lax.all_to_all(
        jnp.broadcast_to(shard[None], (count, *shard.shape)), axis, 0, 0, tiled=True
    )


def of_everyone(shard, axis):
    everything = from_everyone(shard, axis)
    return jnp.sum(everything, axis=0)


def packed_total(arrays, axis):
    ravelled, at, outs = (jnp.concatenate([a.reshape(-1) for a in arrays]), 0, [])
    total = of_everyone(ravelled, axis)
    for a in arrays:
        outs.append(total[at : at + a.size].reshape(a.shape))
        at += a.size
    return tuple(outs)


def sum_in_order(pieces, axes, order):
    lengths = [lax.axis_size(a) for a in axes]
    pieces = pieces.reshape(*lengths, *pieces.shape[1:])
    pieces = pieces.transpose(*order, *range(len(axes), pieces.ndim))
    pieces = pieces.reshape(-1, *pieces.shape[len(axes) :])
    for k in order:
        pieces = lax.psum_scatter(pieces, axes[k], scatter_dimension=0, tiled=True)
    return pieces[0]


def cut_along(shard, dim, count):
    lengths = shard.shape
    pieces = shard.reshape(*lengths[:dim], count, lengths[dim] // count, *lengths[dim + 1 :])
    return jnp.moveaxis(pieces, dim, 0)


def summed_rows(shard, axes, order, dim):
    count = lax.axis_size(axes)
    return sum_in_order(cut_along(shard, dim, count), axes, order)


def local(context, projected, cotangent, modality, out_weight, out_gain):
    towers = out_weight.shape[1]
    tower_ids = jnp.arange(towers, dtype=jnp.int32)
    onehot = (modality[:, None] == tower_ids[None, :]).astype(jnp.float32)
    proj_float = projected.astype(jnp.float32)
    cot_float = cotangent.astype(jnp.float32)
    gain_tok = jnp.dot(onehot, out_gain, precision=lax.Precision.HIGHEST)
    scaled = cot_float * gain_tok
    squares, raw_inner = packed_total(
        (
            jnp.sum(proj_float * proj_float, axis=1, keepdims=True),
            jnp.sum(scaled * proj_float, axis=1, keepdims=True),
        ),
        DP,
    )
    inverse_rms = lax.rsqrt(squares / D + EPS)
    normed = proj_float * inverse_rms
    inner = inverse_rms * raw_inner
    gain_terms = jnp.dot(onehot.T, cot_float * normed, precision=lax.Precision.HIGHEST)
    grad_gain = of_everyone(gain_terms, "shard")
    grad_proj = (inverse_rms * (scaled - normed * (inner / D))).astype(jnp.bfloat16)
    column_rows = lax.all_to_all(context, "shard", split_axis=1, concat_axis=0, tiled=True)
    row_count = out_weight.shape[0]
    piece_grad = lax.all_gather(grad_proj, "shard", axis=0, tiled=True)
    piece_ids = lax.all_gather(modality, "shard", axis=0, tiled=True)
    count = piece_grad.shape[0]
    piece_partial = jnp.zeros((count, row_count), jnp.float32)
    updated = []
    for member in range(towers):
        chosen = piece_ids[:, None] == member
        product = lax.dot_general(
            piece_grad,
            out_weight[:, member, :],
            (((1,), (1,)), ((), ())),
            preferred_element_type=jnp.float32,
        )
        piece_partial = piece_partial + chosen.astype(jnp.float32) * product
        masked = jnp.where(chosen, column_rows, jnp.zeros_like(column_rows))
        updated.append(
            lax.dot_general(
                masked, piece_grad, (((0,), (0,)), ((), ())), preferred_element_type=jnp.float32
            )
        )
    partial_value = piece_partial
    weight_accs, partial_value = (tuple(updated), partial_value)
    grad_weight = jnp.stack(weight_accs, axis=1)
    shard_count = lax.axis_size("shard")
    replica_count = lax.axis_size(DP)
    tok_here = grad_proj.shape[0]
    sub_rows = tok_here // replica_count
    grouped = partial_value.reshape(shard_count, replica_count, sub_rows, row_count)
    reduced = summed_rows(grouped, DP, (1, 0), 1).astype(jnp.bfloat16)
    reduced = reduced.reshape(shard_count, sub_rows, row_count)
    spread = lax.all_to_all(reduced, "shard", split_axis=0, concat_axis=2, tiled=True)
    settled = lax.all_to_all(spread, DP, split_axis=2, concat_axis=1, tiled=True)
    grad_context = settled.reshape(tok_here, settled.shape[2])
    return (grad_context, grad_weight, grad_gain)


def solution(mesh):
    finer = Mesh(mesh.devices.reshape(2, 4, mesh.shape["shard"]), ("dp_0", "dp_1", "shard"))
    return jax.shard_map(
        local,
        mesh=finer,
        in_specs=(
            P("shard", None),
            P("shard", DP),
            P("shard", DP),
            P("shard"),
            P("shard", None, DP),
            P(None, DP),
        ),
        out_specs=(P("shard", DP), P("shard", None, DP), P(None, DP)),
        check_vma=False,
    )
```

profile of v0, /device:TPU:32, one launch (start us, length us, event | category | flops | bytes accessed | tf_op | source)
XLA Modules:
  0.0 406.7 jit_solution(18081353275957798756)
XLA Ops:
  7.2 0.0 copy-start
  7.2 0.0 all-gather.3.cloned.1.call-start
  7.2 0.6 copy-done
  7.9 1.4 fusion.16
  9.3 31.5 %all_to_all.63 = f32[8,1,256]{2,1,0:T(1,128)S(1)} all-to-all(f32[8,1,256]{2,1,0:T(1,128)S(1)} %broadcast_in_dim.35), channel_id=1, replica_groups=mesh['dp_0'=2,'dp_1'=4,'shard'=64] {'dp_0','dp_1'}, dimensions={0} | all-to-all | bytes 16384 | tf_op jit(solution)/shard_map/all_to_all | solution.py:14
  40.9 1.7 fusion.14
  42.6 0.0 all-gather.3.cloned.1.call-update
  42.6 113.4 %all-gather = s32[64,1,128]{2,1,0:T(1,128)S(1)} all-gather(s32[1,1,128]{2,1,0:T(1,128)} %bitcast.89), channel_id=1, replica_groups=mesh['dp_0'=2,'dp_1'=4,'shard'=64] {'shard'}, dimensions={0}, use_global_device_ids=true | all-gather | bytes 33280 | tf_op jit(solution)/shard_map/all_gather | solution.py:78
  156.0 1.3 fusion.15
  157.3 0.9 broadcast_in_dim.39
  158.2 10.1 %all-to-all-start.4 = ((f32[64,3,512]{2,1,0:T(4,128)}), f32[64,3,512]{2,1,0:T(4,128)S(1)}, u32[]{:S(2)}, u32[]{:S(2)}) async-start(f32[64,3,512]{2,1,0:T(4,128)} %broadcast_in_dim.39), calls=%async_computation.6 | async-start | bytes 1048576 | tf_op jit(solution)/shard_map/all_to_all | solution.py:14
  168.2 0.0 reduce-scatter.3.cloned.1.call-start
  168.3 0.0 all-gather.3.cloned.1.call-done
  168.3 0.0 copy-start.1
  168.3 0.0 copy-start.3
  168.3 6.2 %convolution_multiply_fusion = f32[8192,64]{0,1:T(8,128)S(1)} fusion(bf16[8192,512]{1,0:T(8,128)(2,1)} %all-gather.3.cloned.1.call-done, f32[8192]{0:T(1024)S(1)} %get-tuple-element.11, bf16[64,3,512]{2,0,1:T(8,128)(2,1)} %param.10), kind=kOutput, calls=%fused_computation | convolution fusion | flops 537395200 | bytes 10584064 | tf_op jit(solution)/shard_map/dot_general | solution.py:84
  174.5 0.0 copy-done.1
  174.5 0.0 copy-done.3
  174.5 2.6 convolution_multiply_fusion.1
  177.2 2.6 fusion.1
  179.8 2.7 copy.46
  182.5 4.5 %copy.47 = f32[2,4,64,1,16,64]{5,4,2,0,1,3:T(8,128)} copy(f32[2,4,64,1,16,64]{5,4,1,0,2,3:T(8,128)} %bitcast.81) | data formatting | bytes 4194304 | tf_op jit(solution)/shard_map/reshape | solution.py:35
  187.0 0.0 copy-start.2
  187.0 0.0 reduce-scatter.3.cloned.1.call-update
  187.1 1.2 copy-done.2
  188.3 1.3 copy.52
  189.5 6.7 %all-to-all-done.4 = f32[64,3,512]{2,1,0:T(4,128)S(1)} async-done(((f32[64,3,512]{2,1,0:T(4,128)}), f32[64,3,512]{2,1,0:T(4,128)S(1)}, u32[]{:S(2)}, u32[]{:S(2)}) %all-to-all-start.4) | async-done | bytes 393248 | tf_op jit(solution)/shard_map/all_to_all | solution.py:14
  196.3 9.1 %all-to-all-start.3 = ((bf16[128,64,64]{0,2,1:T(8,128)(2,1)}), bf16[128,64,64]{0,2,1:T(8,128)(2,1)S(1)}, u32[]{:S(2)}, u32[]{:S(2)}) async-start(bf16[128,64,64]{0,2,1:T(8,128)(2,1)} %bitcast.20), calls=%async_computation.5 | async-start | bytes 2097152 | tf_op jit(solution)/shard_map/all_to_all | solution.py:75
  205.4 0.0 reduce-scatter.5.cloned.1.call-start
  205.5 33.3 %reduce-scatter.3.cloned.1.call-done = f32[2,64,1,16,64]{4,3,1,0,2:T(8,128)} async-done(((f32[8,64,1,16,64]{4,3,1,0,2:T(8,128)}), f32[2,64,1,16,64]{4,3,1,0,2:T(8,128)}) %reduce-scatter.3.cloned.1.call-update) | async-done | bytes 524304 | tf_op jit(solution)/shard_map/reduce_scatter | solution.py:39
  238.8 0.0 reduce-scatter.5.cloned.1.call-update
  238.8 0.7 reduce_sum.39
  239.5 15.5 %all-to-all-done.3 = bf16[128,64,64]{0,2,1:T(8,128)(2,1)S(1)} async-done(((bf16[128,64,64]{0,2,1:T(8,128)(2,1)}), bf16[128,64,64]{0,2,1:T(8,128)(2,1)S(1)}, u32[]{:S(2)}, u32[]{:S(2)}) %all-to-all-start.3) | async-done | bytes 1048608 | tf_op jit(solution)/shard_map/all_to_all | solution.py:75
  255.1 5.3 %convolution_bitcast_fusion = f32[64,1,512]{2,0,1:T(8,128)S(1)} fusion(bf16[8192,512]{1,0:T(8,128)(2,1)} %all-gather.3.cloned.1.call-done, pred[8192]{0:T(1024)(128)(4,1)S(1)} %get-tuple-element.12, bf16[128,64,64]{0,2,1:T(8,128)(2,1)S(1)} %all-to-all-done.3), kind=kOutput, calls=%fused_computation.6 | convolution fusion | flops 537395200 | bytes 9576448 | tf_op jit(solution)/shard_map/dot_general | solution.py:93
  260.3 46.1 %reduce-scatter.5.cloned.1.call-done = f32[1,64,1,16,64]{4,3,1,0,2:T(8,128)} async-done(((f32[2,64,1,16,64]{4,3,1,0,2:T(8,128)}), f32[1,64,1,16,64]{4,3,1,0,2:T(8,128)}) %reduce-scatter.5.cloned.1.call-update) | async-done | bytes 262160 | tf_op jit(solution)/shard_map/reduce_scatter | solution.py:39
  306.4 1.1 convert_bitcast_fusion
  307.5 0.9 reshape.65
  308.3 14.9 %all-to-all-start.1 = ((bf16[64,2,512]{2,1,0:T(2,128)(2,1)}), bf16[64,2,512]{2,1,0:T(2,128)(2,1)S(1)}, u32[]{:S(2)}, u32[]{:S(2)}) async-start(bf16[64,2,512]{2,1,0:T(2,128)(2,1)} %reshape.65), calls=%async_computation.3 | async-start | bytes 262144 | tf_op jit(solution)/shard_map/all_to_all | solution.py:107
  323.2 4.9 %convolution_bitcast_fusion.1 = f32[64,1,512]{2,0,1:T(8,128)S(1)} fusion(bf16[8192,512]{1,0:T(8,128)(2,1)} %all-gather.3.cloned.1.call-done, pred[8192]{0:T(1024)(128)(4,1)S(1)} %get-tuple-element.14, bf16[128,64,64]{0,2,1:T(8,128)(2,1)S(1)} %all-to-all-done.3), kind=kOutput, calls=%fused_computation.7 | convolution fusion | flops 537395200 | bytes 9576448 | tf_op jit(solution)/shard_map/dot_general | solution.py:93
  328.1 8.7 %all-to-all-done.1 = bf16[64,2,512]{2,1,0:T(2,128)(2,1)S(1)} async-done(((bf16[64,2,512]{2,1,0:T(2,128)(2,1)}), bf16[64,2,512]{2,1,0:T(2,128)(2,1)S(1)}, u32[]{:S(2)}, u32[]{:S(2)}) %all-to-all-start.1) | async-done | bytes 131104 | tf_op jit(solution)/shard_map/all_to_all | solution.py:107
  336.9 0.2 reshape.66
  337.1 0.1 copy.48
  337.2 0.3 all_to_all.49
  337.4 2.7 copy.49
  340.2 0.5 broadcast.57
  340.7 23.5 %reduce.1 = bf16[4096,16]{1,0:T(8,128)(2,1)} reduce(bf16[4096,1,16]{2,1,0:T(2,128)(2,1)S(1)} %bitcast.82, bf16[]{:T(256)} %broadcast.57), dimensions={1}, to_apply=%bitcast.58.reduce_sub_computation | reduce | bytes 262146
  364.2 3.1 reshape.67
  367.3 10.1 %all-to-all-start.2 = ((bf16[8,2,4096]{2,1,0:T(2,128)(2,1)}), bf16[8,2,4096]{2,1,0:T(2,128)(2,1)S(1)}, u32[]{:S(2)}, u32[]{:S(2)}) async-start(bf16[8,2,4096]{2,1,0:T(2,128)(2,1)} %reshape.67), calls=%async_computation.4 | async-start | bytes 262144 | tf_op jit(solution)/shard_map/all_to_all | solution.py:108
  377.3 4.9 %convolution_bitcast_fusion.2 = f32[64,1,512]{2,0,1:T(8,128)S(1)} fusion(bf16[8192,512]{1,0:T(8,128)(2,1)} %all-gather.3.cloned.1.call-done, pred[8192]{0:T(1024)(128)(4,1)S(1)} %get-tuple-element.6, bf16[128,64,64]{0,2,1:T(8,128)(2,1)S(1)} %all-to-all-done.3), kind=kOutput, calls=%fused_computation.8 | convolution fusion | flops 537395200 | bytes 9576448 | tf_op jit(solution)/shard_map/dot_general | solution.py:93
  382.3 0.8 pad_maximum_fusion
  383.0 12.6 %all-to-all-done.2 = bf16[8,2,4096]{2,1,0:T(2,128)(2,1)S(1)} async-done(((bf16[8,2,4096]{2,1,0:T(2,128)(2,1)}), bf16[8,2,4096]{2,1,0:T(2,128)(2,1)S(1)}, u32[]{:S(2)}, u32[]{:S(2)}) %all-to-all-start.2) | async-done | bytes 131104 | tf_op jit(solution)/shard_map/all_to_all | solution.py:108
  395.6 1.8 reshape.68
  397.4 2.0 copy.50
  399.5 0.7 copy.51
  (7 shorter events, 0.1 us)
Async XLA Ops:
  7.2 0.7 copy-start
  7.2 161.1 %all-gather.3.cloned.1.call-start = ((), (), s32[]{:S(2)}) async-start(), calls=%async_computation.7 | async-start | bytes 8519680 | tf_op jit(solution)/shard_map/all_gather | solution.py:77
  158.2 38.1 %all-to-all-start.4 = ((f32[64,3,512]{2,1,0:T(4,128)}), f32[64,3,512]{2,1,0:T(4,128)S(1)}, u32[]{:S(2)}, u32[]{:S(2)}) async-start(f32[64,3,512]{2,1,0:T(4,128)} %broadcast_in_dim.39), calls=%async_computation.6 | async-start | bytes 1048576 | tf_op jit(solution)/shard_map/all_to_all | solution.py:14
  168.2 70.5 %reduce-scatter.3.cloned.1.call-start = ((), (), s32[]{:S(2)}) async-start(), calls=%async_computation.8 | async-start | bytes 5242880 | tf_op jit(solution)/shard_map/reduce_scatter | solution.py:39
  168.3 6.2 %copy-start.1 = (bf16[8192,512]{1,0:T(8,128)(2,1)S(1)}, bf16[8192,512]{1,0:T(8,128)(2,1)}, u32[]{:S(2)}) copy-start(bf16[8192,512]{1,0:T(8,128)(2,1)} %all-gather.3.cloned.1.call-done) | copy-start | bytes 25165828
  168.3 6.2 %copy-start.3 = (bf16[64,3,512]{2,0,1:T(8,128)(2,1)S(1)}, bf16[64,3,512]{2,0,1:T(8,128)(2,1)}, u32[]{:S(2)}) copy-start(bf16[64,3,512]{2,0,1:T(8,128)(2,1)} %param.10) | copy-start | bytes 589828
  187.0 1.2 copy-start.2
  196.3 58.8 %all-to-all-start.3 = ((bf16[128,64,64]{0,2,1:T(8,128)(2,1)}), bf16[128,64,64]{0,2,1:T(8,128)(2,1)S(1)}, u32[]{:S(2)}, u32[]{:S(2)}) async-start(bf16[128,64,64]{0,2,1:T(8,128)(2,1)} %bitcast.20), calls=%async_computation.5 | async-start | bytes 2097152 | tf_op jit(solution)/shard_map/all_to_all | solution.py:75
  205.4 101.0 %reduce-scatter.5.cloned.1.call-start = ((), (), s32[]{:S(2)}) async-start(), calls=%async_computation.9 | async-start | bytes 1572864 | tf_op jit(solution)/shard_map/reduce_scatter | solution.py:39
  308.3 28.5 %all-to-all-start.1 = ((bf16[64,2,512]{2,1,0:T(2,128)(2,1)}), bf16[64,2,512]{2,1,0:T(2,128)(2,1)S(1)}, u32[]{:S(2)}, u32[]{:S(2)}) async-start(bf16[64,2,512]{2,1,0:T(2,128)(2,1)} %reshape.65), calls=%async_computation.3 | async-start | bytes 262144 | tf_op jit(solution)/shard_map/all_to_all | solution.py:107
  367.3 28.3 %all-to-all-start.2 = ((bf16[8,2,4096]{2,1,0:T(2,128)(2,1)}), bf16[8,2,4096]{2,1,0:T(2,128)(2,1)S(1)}, u32[]{:S(2)}, u32[]{:S(2)}) async-start(bf16[8,2,4096]{2,1,0:T(2,128)(2,1)} %reshape.67), calls=%async_computation.4 | async-start | bytes 262144 | tf_op jit(solution)/shard_map/all_to_all | solution.py:108
Sparse Core Ops, SparseCore 0:
  42.7 119.8 all-gather.2
  187.2 51.5 reduce-scatter.2
  241.6 64.7 reduce-scatter.4
where the time goes:
time: 408 us; the launch traced here: 407 us
  blocking collectives  145 us (36%)
  waiting for transfers between devices  123 us (30%)
  starting transfers between devices  44.3 us (11%)
  matrix products  29.2 us (7%)
  other arithmetic  27.8 us (7%)
  local copies, waits for them, and re-layouts  23.6 us (6%)
  between operations  13.9 us (3%)
    all_gather x1, blocking collectives, local(): piece_ids = lax.all_gather(modality, 'shard', axis=0, tiled=True)  113 us
    reduce_scatter x2, waiting for transfers between devices, sum_in_order(): pieces = lax.psum_scatter(pieces, axes[k], scatter_dimension=0, tiled=True)  79.4 us
    all_to_all x1, blocking collectives, from_everyone(): lax.all_to_all(jnp.broadcast_to(shard[None], (count, *shard.shape)), axis...  31.5 us
    unnamed x1, other arithmetic  23.5 us
    all_to_all x1, waiting for transfers between devices, local(): lax.all_to_all(context, 'shard', split_axis=1, concat_axis=0, tiled=True)  15.5 us
    dot_general x3, matrix products, local(): lax.dot_general(masked, piece_grad, (((0,), (0,)), ((), ())), preferred_e...  15.1 us
    all_to_all x1, starting transfers between devices, local(): lax.all_to_all(reduced, 'shard', split_axis=0, concat_axis=2, tiled=True)  14.9 us
    all_to_all x1, waiting for transfers between devices, local(): lax.all_to_all(spread, DP, split_axis=2, concat_axis=1, tiled=True)  12.6 us
  transfers between devices with their start and end apart: 7, of which 6 were waited for; matrix products, arithmetic and copies ran while one was open for 10% of the time, Pallas kernels for 0%

commit v1 on v0

--- a/solution.py
+++ b/solution.py
@@ -72,7 +72,10 @@
     gain_terms = jnp.dot(onehot.T, cot_float * normed, precision=lax.Precision.HIGHEST)
     grad_gain = of_everyone(gain_terms, "shard")
     grad_proj = (inverse_rms * (scaled - normed * (inner / D))).astype(jnp.bfloat16)
-    column_rows = lax.all_to_all(context, "shard", split_axis=1, concat_axis=0, tiled=True)
+    column_rows = jnp.concatenate(
+        lax.all_to_all(jnp.stack(jnp.split(context, lax.axis_size("shard"), 1), 0), "shard", 0, 0),
+        0,
+    )
     row_count = out_weight.shape[0]
     piece_grad = lax.all_gather(grad_proj, "shard", axis=0, tiled=True)
     piece_ids = lax.all_gather(modality, "shard", axis=0, tiled=True)

time: 408 us -> 452 us (1.11)
  local copies, waits for them, and re-layouts: 23.6 us -> 68.2 us
    unnamed x15 -> x147, local copies, waits for them, and re-layouts: 9.67 us -> 51 us
  transfers between devices with their start and end apart: 7 -> 7, of which waited for: 6 -> 6; matrix products, arithmetic and copies ran while one was open for 10% -> 19% of each run, Pallas kernels for 0% -> 0%
where the time goes in v1:
time: 452 us; the launch traced here: 451 us
  blocking collectives  145 us (32%)
  waiting for transfers between devices  123 us (27%)
  local copies, waits for them, and re-layouts  68.2 us (15%)
  starting transfers between devices  44.4 us (10%)
  matrix products  28.2 us (6%)
  other arithmetic  27.8 us (6%)
  between operations  14.6 us (3%)
    all_gather x1, blocking collectives, local(): piece_ids = lax.all_gather(modality, 'shard', axis=0, tiled=True)  113 us
    reduce_scatter x2, waiting for transfers between devices, sum_in_order(): pieces = lax.psum_scatter(pieces, axes[k], scatter_dimension=0, tiled=True)  79.1 us
    unnamed x147, local copies, waits for them, and re-layouts  51 us
    all_to_all x1, blocking collectives, from_everyone(): lax.all_to_all(jnp.broadcast_to(shard[None], (count, *shard.shape)), axis...  31.5 us
    unnamed x1, other arithmetic  23.5 us
    all_to_all x1, waiting for transfers between devices, local(): lax.all_to_all(jnp.stack(jnp.split(context, lax.axis_size('shard'), 1), 0...  15.6 us
    dot_general x3, matrix products, local(): lax.dot_general(masked, piece_grad, (((0,), (0,)), ((), ())), preferred_e...  15.1 us
    all_to_all x1, starting transfers between devices, local(): lax.all_to_all(reduced, 'shard', split_axis=0, concat_axis=2, tiled=True)  15.1 us
  transfers between devices with their start and end apart: 7, of which 6 were waited for; matrix products, arithmetic and copies ran while one was open for 19% of the time, Pallas kernels for 0%

profile of v1, /device:TPU:32, one launch (start us, length us, event | category | flops | bytes accessed | tf_op | source)
XLA Modules:
  0.0 451.2 jit_solution(15223505715291028042)
XLA Ops:
  7.2 0.6 copy-done
  7.9 1.4 fusion.16
  9.3 31.5 %all_to_all.49 = f32[8,1,256]{2,1,0:T(1,128)S(1)} all-to-all(f32[8,1,256]{2,1,0:T(1,128)S(1)} %broadcast_in_dim.35), channel_id=1, replica_groups=mesh['dp_0'=2,'dp_1'=4,'shard'=64] {'dp_0','dp_1'}, dimensions={0} | all-to-all | bytes 16384 | tf_op jit(solution)/shard_map/all_to_all | solution.py:14
  40.9 1.7 fusion.14
  42.6 1.0 fusion.36
  44.3 1.3 fusion.35
  51.6 113.3 %all-gather = s32[64,1,128]{2,1,0:T(1,128)S(1)} all-gather(s32[1,1,128]{2,1,0:T(1,128)S(1)} %bitcast.215), channel_id=1, replica_groups=mesh['dp_0'=2,'dp_1'=4,'shard'=64] {'shard'}, dimensions={0}, use_global_device_ids=true | all-gather | bytes 33280 | tf_op jit(solution)/shard_map/all_gather | solution.py:81
  164.9 0.6 constant_dynamic-update-slice_fusion.63
  166.7 0.6 constant_dynamic-update-slice_fusion.60
  168.5 0.6 constant_dynamic-update-slice_fusion.57
  169.1 0.6 constant_dynamic-update-slice_fusion.56
  170.9 0.6 constant_dynamic-update-slice_fusion.53
  171.5 0.6 constant_dynamic-update-slice_fusion.52
  173.9 0.6 constant_dynamic-update-slice_fusion.48
  174.5 0.6 constant_dynamic-update-slice_fusion.47
  176.3 0.6 constant_dynamic-update-slice_fusion.44
  177.5 0.6 constant_dynamic-update-slice_fusion.42
  178.7 0.6 constant_dynamic-update-slice_fusion.40
  179.9 0.6 constant_dynamic-update-slice_fusion.38
  182.9 0.6 constant_dynamic-update-slice_fusion.33
  184.1 0.6 constant_dynamic-update-slice_fusion.31
  185.3 0.6 constant_dynamic-update-slice_fusion.29
  186.5 0.6 constant_dynamic-update-slice_fusion.27
  190.1 0.6 constant_dynamic-update-slice_fusion.21
  190.7 0.6 constant_dynamic-update-slice_fusion.20
  193.7 0.6 constant_dynamic-update-slice_fusion.15
  194.9 0.6 constant_dynamic-update-slice_fusion.13
  195.5 0.6 constant_dynamic-update-slice_fusion.12
  197.3 0.6 constant_dynamic-update-slice_fusion.9
  198.5 0.6 constant_dynamic-update-slice_fusion.7
  199.1 0.6 constant_dynamic-update-slice_fusion.6
  199.7 0.6 constant_dynamic-update-slice_fusion.5
  200.3 0.6 constant_dynamic-update-slice_fusion.4
  201.9 0.9 broadcast_in_dim.39
  202.8 10.0 %all-to-all-start.4 = ((f32[64,3,512]{2,1,0:T(4,128)}), f32[64,3,512]{2,1,0:T(4,128)S(1)}, u32[]{:S(2)}, u32[]{:S(2)}) async-start(f32[64,3,512]{2,1,0:T(4,128)} %broadcast_in_dim.39), calls=%async_computation.6 | async-start | bytes 1048576 | tf_op jit(solution)/shard_map/all_to_all | solution.py:14
  212.9 6.2 %convolution_multiply_fusion = f32[8192,64]{0,1:T(8,128)S(1)} fusion(bf16[8192,512]{1,0:T(8,128)(2,1)} %all-gather.3.cloned.1.call-done, f32[8192]{0:T(1024)S(1)} %get-tuple-element.75, bf16[64,3,512]{2,0,1:T(8,128)(2,1)S(1)} %copy-done.4), kind=kOutput, calls=%fused_computation | convolution fusion | flops 537395200 | bytes 10584064 | tf_op jit(solution)/shard_map/dot_general | solution.py:87
  219.1 2.6 convolution_multiply_fusion.1
  221.7 2.6 fusion.1
  224.3 2.7 copy.241
  227.0 4.6 %copy.242 = f32[2,4,64,1,16,64]{5,4,2,0,1,3:T(8,128)} copy(f32[2,4,64,1,16,64]{5,4,1,0,2,3:T(8,128)} %bitcast.207) | data formatting | bytes 4194304 | tf_op jit(solution)/shard_map/reshape | solution.py:35
  231.6 0.6 constant_dynamic-update-slice_fusion.2
  232.4 0.6 constant_dynamic-update-slice_fusion.1
  233.6 7.2 %all-to-all-done.4 = f32[64,3,512]{2,1,0:T(4,128)S(1)} async-done(((f32[64,3,512]{2,1,0:T(4,128)}), f32[64,3,512]{2,1,0:T(4,128)S(1)}, u32[]{:S(2)}, u32[]{:S(2)}) %all-to-all-start.4) | async-done | bytes 393248 | tf_op jit(solution)/shard_map/all_to_all | solution.py:14
  240.8 9.1 %all-to-all-start.3 = ((bf16[64,128,64]{1,2,0:T(8,128)(2,1)}), bf16[64,128,64]{1,2,0:T(8,128)(2,1)S(1)}, u32[]{:S(2)}, u32[]{:S(2)}) async-start(bf16[64,128,64]{1,2,0:T(8,128)(2,1)} %constant_dynamic-update-slice_fusion), calls=%async_computation.5 | async-start | bytes 2097152 | tf_op jit(solution)/shard_map/all_to_all | solution.py:76
  250.2 33.1 %reduce-scatter.3.cloned.1.call-done = f32[2,64,1,16,64]{4,3,1,0,2:T(8,128)} async-done(((f32[8,64,1,16,64]{4,3,1,0,2:T(8,128)}), f32[2,64,1,16,64]{4,3,1,0,2:T(8,128)}) %reduce-scatter.3.cloned.1.call-update) | async-done | bytes 524304 | tf_op jit(solution)/shard_map/reduce_scatter | solution.py:39
  283.3 0.7 reduce_sum.39
  284.0 15.6 %all-to-all-done.3 = bf16[64,128,64]{1,2,0:T(8,128)(2,1)S(1)} async-done(((bf16[64,128,64]{1,2,0:T(8,128)(2,1)}), bf16[64,128,64]{1,2,0:T(8,128)(2,1)S(1)}, u32[]{:S(2)}, u32[]{:S(2)}) %all-to-all-start.3) | async-done | bytes 1048608 | tf_op jit(solution)/shard_map/all_to_all | solution.py:76
  299.6 5.3 %convolution_bitcast_fusion.2 = f32[64,1,512]{2,0,1:T(8,128)S(1)} fusion(bf16[8192,512]{1,0:T(8,128)(2,1)} %all-gather.3.cloned.1.call-done, pred[8192]{0:T(1024)(128)(4,1)S(1)} %get-tuple-element.6, bf16[64,128,64]{1,2,0:T(8,128)(2,1)S(1)} %all-to-all-done.3), kind=kOutput, calls=%fused_computation.8 | convolution fusion | flops 537395200 | bytes 9576448 | tf_op jit(solution)/shard_map/dot_general | solution.py:96
  304.9 46.0 %reduce-scatter.5.cloned.1.call-done = f32[1,64,1,16,64]{4,3,1,0,2:T(8,128)} async-done(((f32[2,64,1,16,64]{4,3,1,0,2:T(8,128)}), f32[1,64,1,16,64]{4,3,1,0,2:T(8,128)}) %reduce-scatter.5.cloned.1.call-update) | async-done | bytes 262160 | tf_op jit(solution)/shard_map/reduce_scatter | solution.py:39
  350.9 1.1 convert_bitcast_fusion
  352.0 0.9 reshape.66
  352.9 15.1 %all-to-all-start.1 = ((bf16[64,2,512]{2,1,0:T(2,128)(2,1)}), bf16[64,2,512]{2,1,0:T(2,128)(2,1)S(1)}, u32[]{:S(2)}, u32[]{:S(2)}) async-start(bf16[64,2,512]{2,1,0:T(2,128)(2,1)} %reshape.66), calls=%async_computation.3 | async-start | bytes 262144 | tf_op jit(solution)/shard_map/all_to_all | solution.py:110
  368.0 4.9 %convolution_bitcast_fusion.1 = f32[64,1,512]{2,0,1:T(8,128)S(1)} fusion(bf16[8192,512]{1,0:T(8,128)(2,1)} %all-gather.3.cloned.1.call-done, pred[8192]{0:T(1024)(128)(4,1)S(1)} %get-tuple-element.78, bf16[64,128,64]{1,2,0:T(8,128)(2,1)S(1)} %all-to-all-done.3), kind=kOutput, calls=%fused_computation.7 | convolution fusion | flops 537395200 | bytes 9576448 | tf_op jit(solution)/shard_map/dot_general | solution.py:96
  372.9 8.7 %all-to-all-done.1 = bf16[64,2,512]{2,1,0:T(2,128)(2,1)S(1)} async-done(((bf16[64,2,512]{2,1,0:T(2,128)(2,1)}), bf16[64,2,512]{2,1,0:T(2,128)(2,1)S(1)}, u32[]{:S(2)}, u32[]{:S(2)}) %all-to-all-start.1) | async-done | bytes 131104 | tf_op jit(solution)/shard_map/all_to_all | solution.py:110
  382.2 2.7 copy.244
  385.4 23.5 %reduce.1 = bf16[4096,16]{1,0:T(8,128)(2,1)} reduce(bf16[4096,1,16]{2,1,0:T(2,128)(2,1)S(1)} %bitcast.208, bf16[]{:T(256)} %broadcast.57), dimensions={1}, to_apply=%bitcast.184.reduce_sub_computation | reduce | bytes 262146
  408.9 3.1 reshape.68
  412.0 9.8 %all-to-all-start.2 = ((bf16[8,2,4096]{2,1,0:T(2,128)(2,1)}), bf16[8,2,4096]{2,1,0:T(2,128)(2,1)S(1)}, u32[]{:S(2)}, u32[]{:S(2)}) async-start(bf16[8,2,4096]{2,1,0:T(2,128)(2,1)} %reshape.68), calls=%async_computation.4 | async-start | bytes 262144 | tf_op jit(solution)/shard_map/all_to_all | solution.py:111
  421.8 4.9 %convolution_bitcast_fusion = f32[64,1,512]{2,0,1:T(8,128)S(1)} fusion(bf16[8192,512]{1,0:T(8,128)(2,1)} %all-gather.3.cloned.1.call-done, pred[8192]{0:T(1024)(128)(4,1)S(1)} %get-tuple-element.76, bf16[64,128,64]{1,2,0:T(8,128)(2,1)S(1)} %all-to-all-done.3), kind=kOutput, calls=%fused_computation.6 | convolution fusion | flops 537395200 | bytes 9576448 | tf_op jit(solution)/shard_map/dot_general | solution.py:96
  426.8 0.8 pad_maximum_fusion
  427.5 12.6 %all-to-all-done.2 = bf16[8,2,4096]{2,1,0:T(2,128)(2,1)S(1)} async-done(((bf16[8,2,4096]{2,1,0:T(2,128)(2,1)}), bf16[8,2,4096]{2,1,0:T(2,128)(2,1)S(1)}, u32[]{:S(2)}, u32[]{:S(2)}) %all-to-all-start.2) | async-done | bytes 131104 | tf_op jit(solution)/shard_map/all_to_all | solution.py:111
  440.1 1.8 reshape.69
  441.9 2.0 copy.245
  444.0 0.7 copy.246
  (134 shorter events, 29.8 us)
Async XLA Ops:
  7.2 0.7 copy-start
  7.2 44.4 %copy-start.6 = (s32[128]{0:T(128)S(1)}, s32[128]{0:T(128)}, u32[]{:S(2)}) copy-start(s32[128]{0:T(128)} %param.9) | copy-start | bytes 1540
  7.2 40.3 %copy-start.2 = (bf16[128,4096]{1,0:T(8,128)(2,1)S(1)}, bf16[128,4096]{1,0:T(8,128)(2,1)}, u32[]{:S(2)}) copy-start(bf16[128,4096]{1,0:T(8,128)(2,1)} %param.6) | copy-start | bytes 3145732
  7.2 205.7 %all-gather.3.cloned.1.call-start = ((), (), s32[]{:S(2)}) async-start(), calls=%async_computation.7 | async-start | bytes 8519680 | tf_op jit(solution)/shard_map/all_gather | solution.py:80
  44.3 157.3 %copy-start.3 = (bf16[128,512]{1,0:T(8,128)(2,1)S(1)}, bf16[128,512]{1,0:T(8,128)(2,1)}, u32[]{:S(2)}) copy-start(bf16[128,512]{1,0:T(8,128)(2,1)} %param.7) | copy-start | bytes 393220
  44.3 157.3 %copy-start.5 = (bf16[128,512]{1,0:T(8,128)(2,1)S(1)}, bf16[128,512]{1,0:T(8,128)(2,1)}, u32[]{:S(2)}) copy-start(bf16[128,512]{1,0:T(8,128)(2,1)} %param.8) | copy-start | bytes 393220
  47.5 165.4 %copy-start.4 = (bf16[64,3,512]{2,0,1:T(8,128)(2,1)S(1)}, bf16[64,3,512]{2,0,1:T(8,128)(2,1)}, u32[]{:S(2)}) copy-start(bf16[64,3,512]{2,0,1:T(8,128)(2,1)} %param.10) | copy-start | bytes 589828
  202.8 38.0 %all-to-all-start.4 = ((f32[64,3,512]{2,1,0:T(4,128)}), f32[64,3,512]{2,1,0:T(4,128)S(1)}, u32[]{:S(2)}, u32[]{:S(2)}) async-start(f32[64,3,512]{2,1,0:T(4,128)} %broadcast_in_dim.39), calls=%async_computation.6 | async-start | bytes 1048576 | tf_op jit(solution)/shard_map/all_to_all | solution.py:14
  212.8 70.5 %reduce-scatter.3.cloned.1.call-start = ((), (), s32[]{:S(2)}) async-start(), calls=%async_computation.8 | async-start | bytes 5242880 | tf_op jit(solution)/shard_map/reduce_scatter | solution.py:39
  212.9 6.2 %copy-start.1 = (bf16[8192,512]{1,0:T(8,128)(2,1)S(1)}, bf16[8192,512]{1,0:T(8,128)(2,1)}, u32[]{:S(2)}) copy-start(bf16[8192,512]{1,0:T(8,128)(2,1)} %all-gather.3.cloned.1.call-done) | copy-start | bytes 25165828
  240.8 58.8 %all-to-all-start.3 = ((bf16[64,128,64]{1,2,0:T(8,128)(2,1)}), bf16[64,128,64]{1,2,0:T(8,128)(2,1)S(1)}, u32[]{:S(2)}, u32[]{:S(2)}) async-start(bf16[64,128,64]{1,2,0:T(8,128)(2,1)} %constant_dynamic-update-slice_fusion), calls=%async_computation.5 | async-start | bytes 2097152 | tf_op jit(solution)/shard_map/all_to_all | solution.py:76
  250.0 100.9 %reduce-scatter.5.cloned.1.call-start = ((), (), s32[]{:S(2)}) async-start(), calls=%async_computation.9 | async-start | bytes 1572864 | tf_op jit(solution)/shard_map/reduce_scatter | solution.py:39
  352.9 28.7 %all-to-all-start.1 = ((bf16[64,2,512]{2,1,0:T(2,128)(2,1)}), bf16[64,2,512]{2,1,0:T(2,128)(2,1)S(1)}, u32[]{:S(2)}, u32[]{:S(2)}) async-start(bf16[64,2,512]{2,1,0:T(2,128)(2,1)} %reshape.66), calls=%async_computation.3 | async-start | bytes 262144 | tf_op jit(solution)/shard_map/all_to_all | solution.py:110
  412.0 28.1 %all-to-all-start.2 = ((bf16[8,2,4096]{2,1,0:T(2,128)(2,1)}), bf16[8,2,4096]{2,1,0:T(2,128)(2,1)S(1)}, u32[]{:S(2)}, u32[]{:S(2)}) async-start(bf16[8,2,4096]{2,1,0:T(2,128)(2,1)} %reshape.68), calls=%async_computation.4 | async-start | bytes 262144 | tf_op jit(solution)/shard_map/all_to_all | solution.py:111
Sparse Core Ops, SparseCore 0:
  42.7 119.1 all-gather.2
  231.7 51.5 reduce-scatter.2
  286.1 64.7 reduce-scatter.4
